TPU v7x, 32 devices: a whole 2x2x4 slice. The times are simulated.
32 devices in a mesh: dp: 2 (over x), expert: 16 (over z, y, core).
Axes of the slice: x: 2, y: 2, z: 4, core: 2. Of those that a mesh axis runs over, the one named last changes fastest.
Arguments:
- q_latent: bfloat16 [128, 16, 576], P(('expert', 'dp')), may hold values from -48 to 48
- latent_cache: bfloat16 [128, 512, 576], P(('expert', 'dp')), may hold values from -10 to 10
- lengths: int32 [128], P(('expert', 'dp')), may hold values from 2 to 512
- residual: bfloat16 [128, 2048], P(('expert', 'dp')), may hold values from -6 to 6
- adapter_ids: int32 [128], P(('expert', 'dp')), may hold values from 0 to 31
- value_out: bfloat16 [8192, 2048], P('expert'), may hold values from -0.0625 to 0.0625
- adapter_down: bfloat16 [8192, 512], P('expert'), may hold values from -0.0625 to 0.0625
- adapter_up_factors: bfloat16 [512, 2048], P('expert'), may hold values from -1.5 to 1.5
- norm_gain: bfloat16 [2048], replicated, may hold values from 0.099609375 to 1.8984375
- expert_ids: int32 [128, 6], P('expert'), may hold values from 0 to 15, all different within a row; in each aligned block of 8 rows (0 to 7, 8 to 15, ...) at most 6 rows name the same one
- gate_weights: float32 [128, 6], P('expert'), may hold values from 0.05 to 0.5
- w_gate: bfloat16 [16, 2048, 1024], P('expert', None, 'dp'), may hold values from -0.125 to 0.125
- w_up: bfloat16 [16, 2048, 1024], P('expert', None, 'dp'), may hold values from -0.125 to 0.125
- w_down: bfloat16 [16, 2048, 1024], P('expert', None, 'dp'), may hold values from -0.1875 to 0.1875
Outputs:
- layer_out: bfloat16 [128, 2048], P(('expert', 'dp'))
Inputs may be any that keep to these rules, and one draw needn't show every extreme that they name: `expert_ids`: each row names 6 different experts. Requests e * 8 to e * 8 + 7 form aligned blocks; in each block no expert is named by more than 6 rows, and in some block an expert is named by exactly 6 rows.
All inputs are finite; a program needn't handle non-finite values.
Results may differ from a plain program's by a relative error of at most 0.008.
Values may be sent and summed in bfloat16 or wider, within the bound.
A program may use at most 64 MiB of HBM per device.

v0:
```python
import jax
import jax.numpy as jnp
from jax import lax
from jax.sharding import PartitionSpec as P

LAT = 512
ADAPTER_RANK = 16
SOFTMAX_SCALE = 192.0 ** (-0.5)
ADAPTER_SCALE = 2.0
EPSILON = 1e-06


def attend_one(query, latent_rows, length):
    scores = (
        lax.dot_general(
            query, latent_rows, (((1,), (1,)), ((), ())), preferred_element_type=jnp.float32
        )
        * SOFTMAX_SCALE
    )
    valid_mask = jnp.arange(latent_rows.shape[0], dtype=jnp.int32) < length
    scores = jnp.where(valid_mask[None, :], scores, -1e30)
    row_max = jnp.max(scores, axis=1, keepdims=True)
    raised = jnp.exp(scores - row_max)
    weights_bf = (raised / jnp.sum(raised, axis=1, keepdims=True)).astype(jnp.bfloat16)
    return jnp.dot(weights_bf, latent_rows[:, :LAT], preferred_element_type=jnp.float32).astype(
        jnp.bfloat16
    )


def expert_rows(tokens, gate_part, up_part, down_part):
    gate_act = jnp.dot(tokens, gate_part, preferred_element_type=jnp.float32)
    up_act = jnp.dot(tokens, up_part, preferred_element_type=jnp.float32)
    hidden_bf = (jax.nn.silu(gate_act) * up_act).astype(jnp.bfloat16)
    return lax.dot_general(
        hidden_bf, down_part, (((1,), (1,)), ((), ())), preferred_element_type=jnp.float32
    )


def local(
    q_latent,
    latent_cache,
    lengths,
    residual,
    adapter_ids,
    value_out,
    adapter_down,
    adapter_up_factors,
    norm_gain,
    expert_ids,
    gate_weights,
    w_gate,
    w_up,
    w_down,
):
    requests = residual.shape[0]
    model_width = residual.shape[1]
    head_count = q_latent.shape[1]
    latent_out = jax.vmap(attend_one)(q_latent, latent_cache, lengths).reshape(
        requests, head_count * LAT
    )
    pieces = lax.all_to_all(latent_out, "expert", split_axis=1, concat_axis=0, tiled=True)
    group_ids = lax.all_gather(adapter_ids, "expert", axis=0, tiled=True)
    group_rows = pieces.shape[0]
    adapters = adapter_down.shape[1] // ADAPTER_RANK
    owned_count = adapter_up_factors.shape[0] // ADAPTER_RANK
    down_projected_rows = jnp.dot(pieces, adapter_down, preferred_element_type=jnp.float32).reshape(
        group_rows, adapters, ADAPTER_RANK
    )
    chosen_adapters = group_ids[:, None] == jnp.arange(adapters, dtype=jnp.int32)[None, :]
    adapter_output = jnp.sum(
        jnp.where(chosen_adapters[:, :, None], down_projected_rows, 0.0), axis=1
    )
    adapter_down_rows = lax.psum(adapter_output, "expert")
    adapter_scaled_output = (ADAPTER_SCALE * adapter_down_rows).astype(jnp.bfloat16)
    first_owned = lax.axis_index("expert") * owned_count
    holder_mask = (
        group_ids[:, None] == first_owned + jnp.arange(owned_count, dtype=jnp.int32)[None, :]
    )
    spread_rows = jnp.where(
        holder_mask[:, :, None], adapter_scaled_output[:, None, :], jnp.zeros((), jnp.bfloat16)
    ).reshape(group_rows, owned_count * ADAPTER_RANK)
    attention = lax.psum_scatter(
        jnp.dot(pieces, value_out, preferred_element_type=jnp.float32)
        + jnp.dot(spread_rows, adapter_up_factors, preferred_element_type=jnp.float32),
        "expert",
        scatter_dimension=0,
        tiled=True,
    )
    residual_flow = residual.astype(jnp.float32) + attention
    inverse_rms = lax.rsqrt(
        jnp.mean(residual_flow * residual_flow, axis=1, keepdims=True) + EPSILON
    )
    normed = (residual_flow * inverse_rms * norm_gain.astype(jnp.float32)).astype(jnp.bfloat16)
    column = lax.all_gather(normed, "dp", axis=0, tiled=True)
    tokens = column.shape[0]
    top_count = expert_ids.shape[1]
    experts = lax.axis_size("expert") * w_gate.shape[0]
    share_size = max(1, 2 * requests * top_count // experts)
    dp_count = lax.axis_size("dp")
    slot_count = share_size * dp_count
    member = expert_ids[:, :, None] == jnp.arange(experts, dtype=jnp.int32)[None, None, :]
    flat_hits = member.reshape(tokens * top_count, experts).astype(jnp.int32)
    slot_rank = jnp.sum((jnp.cumsum(flat_hits, axis=0) - 1) * flat_hits, axis=1).reshape(
        tokens, top_count
    )
    placed = member[:, :, :, None] & (
        slot_rank[:, :, None, None] == jnp.arange(slot_count, dtype=jnp.int32)[None, None, None, :]
    )
    routing = jnp.any(placed, axis=1).reshape(tokens, experts * slot_count)
    combine = jnp.sum(jnp.where(placed, gate_weights[:, :, None, None], 0.0), axis=1).reshape(
        tokens, experts * slot_count
    )
    routing_rows = routing.T.astype(jnp.bfloat16)
    outgoing = (
        jnp.dot(routing_rows, column, preferred_element_type=jnp.float32)
        .astype(jnp.bfloat16)
        .reshape(experts, slot_count, model_width)
    )
    arrived = lax.all_to_all(outgoing, "expert", split_axis=0, concat_axis=0, tiled=True)
    produced = expert_rows(arrived.reshape(-1, model_width), w_gate[0], w_up[0], w_down[0])
    partial_value = produced.reshape(arrived.shape[0], arrived.shape[1], model_width)
    returned = lax.all_to_all(
        partial_value.astype(jnp.bfloat16), "expert", split_axis=0, concat_axis=0, tiled=True
    ).astype(partial_value.dtype)
    routed_column = jnp.dot(
        combine,
        returned.reshape(experts * slot_count, model_width),
        precision=lax.Precision.HIGHEST,
        preferred_element_type=jnp.float32,
    )
    routed_sum = lax.psum_scatter(
        routed_column.astype(jnp.bfloat16), "dp", scatter_dimension=0, tiled=True
    ).astype(jnp.float32)
    return (residual_flow + routed_sum).astype(jnp.bfloat16)


def solution(mesh):
    in_specs = (
        P(("expert", "dp"), None, None),
        P(("expert", "dp"), None, None),
        P(("expert", "dp")),
        P(("expert", "dp"), None),
        P(("expert", "dp")),
        P("expert", None),
        P("expert", None),
        P("expert", None),
        P(),
        P("expert", None),
        P("expert", None),
        P("expert", None, "dp"),
        P("expert", None, "dp"),
        P("expert", None, "dp"),
    )
    out_specs = P(("expert", "dp"), None)
    return jax.shard_map(local, mesh=mesh, in_specs=in_specs, out_specs=out_specs, check_vma=False)
```

profile of v0, /device:TPU:0, one launch (start us, length us, event | category | flops | bytes accessed | tf_op | source)
XLA Modules:
  0.0 223.4 jit_solution(10527450560244738211)
XLA Ops:
  6.5 0.9 iota_compare_fusion.4
  7.4 2.1 fusion.17
  9.6 0.2 fusion.31
  9.8 2.3 %fusion.19 = bf16[4,16,512]{2,1,0:T(8,128)(2,1)S(1)} fusion(bf16[4,512,576]{1,2,0:T(8,128)(2,1)} %param.15, f32[4,16]{1,0:T(4,128)S(1)} %fusion.31, f32[4,16,512]{2,1,0:T(8,128)S(1)} %fusion.17), kind=kOutput, calls=%fused_computation.21 | convolution fusion | flops 33686080 | bytes 2426880 | tf_op jit(solution)/shard_map/vmap()/dot_general | solution.py:25
  12.1 0.7 copy.29
  12.8 7.4 %all-to-all-start = ((bf16[4,16,512]{2,0,1:T(4,128)(2,1)}), bf16[4,16,512]{2,0,1:T(4,128)(2,1)S(1)}, u32[]{:S(2)}, u32[]{:S(2)}) async-start(bf16[4,16,512]{2,0,1:T(4,128)(2,1)} %copy.29), calls=%async_computation | async-start | bytes 131072 | tf_op jit(solution)/shard_map/all_to_all | solution.py:61
  20.4 0.6 fusion.30
  21.7 0.2 dynamic-update-slice
  21.9 12.4 %all-reduce = s32[64]{0:T(128)S(1)} all-reduce(s32[64]{0:T(128)S(1)} %dynamic-update-slice), channel_id=1, replica_groups=mesh['dp'=2,'expert'=16] {'expert'}, use_global_device_ids=true, to_apply=%add | all-reduce | flops 64 | bytes 512
  34.3 0.2 copy.30
  34.7 0.2 select_reduce_fusion
  35.2 0.5 fusion.16
  35.7 30.0 %psum.7 = f32[64,16]{0,1:T(8,128)S(1)} all-reduce(f32[64,16]{0,1:T(8,128)S(1)} %fusion.16), channel_id=1, replica_groups=mesh['dp'=2,'expert'=16] {'expert'}, use_global_device_ids=true, to_apply=%region_3.4 | all-reduce | flops 1024 | bytes 8192 | tf_op jit(solution)/shard_map/psum | solution.py:73
  65.7 2.1 fusion.32
  67.8 1.1 convolution_add_fusion
  69.1 0.1 copy.35
  70.0 87.0 %all-reduce.5.cloned.1.call-done = f32[64,2048]{1,0:T(8,128)} async-done(((f32[64,2048]{1,0:T(8,128)}), f32[64,2048]{1,0:T(8,128)}) %all-reduce.5.cloned.1.call-update) | async-done | bytes 524304
  157.0 1.0 multiply_reduce_fusion
  158.0 0.9 fusion.28
  158.9 4.4 %all-gather = bf16[2,4,2048]{2,1,0:T(4,128)(2,1)S(1)} all-gather(bf16[1,4,2048]{2,1,0:T(4,128)(2,1)S(1)} %fusion.28), channel_id=1, replica_groups=mesh['dp'=2,'expert'=16] {'dp'}, dimensions={0}, use_global_device_ids=true | all-gather | bytes 49152 | tf_op jit(solution)/shard_map/all_gather | solution.py:94
  163.3 0.3 convolution_convert_fusion.1
  163.8 19.2 %all_to_all.26 = bf16[16,6,2048]{2,1,0:T(8,128)(2,1)S(1)} all-to-all(bf16[16,6,2048]{2,1,0:T(8,128)(2,1)S(1)} %reshape.122), channel_id=1, replica_groups=mesh['dp'=2,'expert'=16] {'expert'}, dimensions={0} | all-to-all | bytes 786432 | tf_op jit(solution)/shard_map/all_to_all | solution.py:119
  183.2 2.2 fusion.5
  185.4 0.5 fusion.13
  186.0 0.8 convolution_convert_fusion
  186.7 1.0 copy.37
  187.8 4.2 %all-to-all-start.2 = ((bf16[16,6,2048]{2,1,0:T(8,128)(2,1)}), bf16[16,6,2048]{2,1,0:T(8,128)(2,1)S(1)}, u32[]{:S(2)}, u32[]{:S(2)}) async-start(bf16[16,6,2048]{2,1,0:T(8,128)(2,1)} %copy.37), calls=%async_computation.2 | async-start | bytes 1048576 | tf_op jit(solution)/shard_map/all_to_all | solution.py:122
  192.0 0.6 dynamic-slice.3
  193.4 12.8 %all-to-all-done.2 = bf16[16,6,2048]{2,1,0:T(8,128)(2,1)S(1)} async-done(((bf16[16,6,2048]{2,1,0:T(8,128)(2,1)}), bf16[16,6,2048]{2,1,0:T(8,128)(2,1)S(1)}, u32[]{:S(2)}, u32[]{:S(2)}) %all-to-all-start.2) | async-done | bytes 393248 | tf_op jit(solution)/shard_map/all_to_all | solution.py:122
  206.2 0.6 fusion.1
  206.8 8.3 %all-reduce.2 = bf16[8,2048]{1,0:T(8,128)(2,1)S(1)} all-reduce(bf16[8,2048]{1,0:T(8,128)(2,1)S(1)} %fusion.1), channel_id=3, replica_groups=mesh['dp'=2,'expert'=16] {'dp'}, use_global_device_ids=true, to_apply=%region_10.11.clone | all-reduce | flops 16384 | bytes 65536
  215.1 1.5 add_convert_fusion
  (51 shorter events, 1.6 us)
Async XLA Ops:
  6.5 179.4 %copy-start = (bf16[1,2048,512]{2,1,0:T(8,128)(2,1)S(1)}, bf16[1,2048,512]{2,1,0:T(8,128)(2,1)}, u32[]{:S(2)}) copy-start(bf16[1,2048,512]{2,1,0:T(8,128)(2,1)} %param.27) | copy-start | bytes 6291460
  9.6 10.7 %copy-start.4 = (s32[8,6]{1,0:T(8,128)S(1)}, s32[8,6]{1,0:T(8,128)}, u32[]{:S(2)}) copy-start(s32[8,6]{1,0:T(8,128)} %param.23) | copy-start | bytes 580
  9.6 10.8 %copy-start.7 = (u32[32]{0:T(128)S(1)}, u32[32]{0:T(128)}, u32[]{:S(2)}) copy-start(u32[32]{0:T(128)} %constant.49) | copy-start | bytes 388
  9.6 12.1 %copy-start.9 = (s32[4]{0:T(128)S(1)}, s32[4]{0:T(128)}, u32[]{:S(2)}) copy-start(s32[4]{0:T(128)} %param.18) | copy-start | bytes 52
  9.6 24.7 %copy-start.1 = (bf16[512,512]{1,0:T(8,128)(2,1)S(1)}, bf16[512,512]{1,0:T(8,128)(2,1)}, u32[]{:S(2)}) copy-start(bf16[512,512]{1,0:T(8,128)(2,1)} %param.20) | copy-start | bytes 1572868
  9.6 25.0 %copy-start.5 = (bf16[2048]{0:T(1024)(128)(2,1)S(1)}, bf16[2048]{0:T(1024)(128)(2,1)}, u32[]{:S(2)}) copy-start(bf16[2048]{0:T(1024)(128)(2,1)} %param.22) | copy-start | bytes 12292
  12.8 22.4 %all-to-all-start = ((bf16[4,16,512]{2,0,1:T(4,128)(2,1)}), bf16[4,16,512]{2,0,1:T(4,128)(2,1)S(1)}, u32[]{:S(2)}, u32[]{:S(2)}) async-start(bf16[4,16,512]{2,0,1:T(4,128)(2,1)} %copy.29), calls=%async_computation | async-start | bytes 131072 | tf_op jit(solution)/shard_map/all_to_all | solution.py:61
  20.2 136.8 %all-reduce.5.cloned.1.call-start = ((), (), s32[]{:S(2)}) async-start(), calls=%async_computation.3 | async-start | bytes 1048576
  34.5 33.3 %copy-start.3 = (bf16[32,2048]{1,0:T(8,128)(2,1)S(1)}, bf16[32,2048]{1,0:T(8,128)(2,1)}, u32[]{:S(2)}) copy-start(bf16[32,2048]{1,0:T(8,128)(2,1)} %param.21) | copy-start | bytes 393220
  65.7 91.3 %copy-start.2 = (bf16[4,2048]{1,0:T(4,128)(2,1)S(1)}, bf16[4,2048]{1,0:T(4,128)(2,1)}, u32[]{:S(2)}) copy-start(bf16[4,2048]{1,0:T(4,128)(2,1)} %param.17) | copy-start | bytes 49156
  183.2 2.2 copy-start.8
  185.9 6.0 %copy-start.6 = (f32[8,6]{1,0:T(8,128)S(1)}, f32[8,6]{1,0:T(8,128)}, u32[]{:S(2)}) copy-start(f32[8,6]{1,0:T(8,128)} %param.24) | copy-start | bytes 580
  185.9 6.1 %copy-start.10 = (u32[32]{0:T(128)S(1)}, u32[32]{0:T(128)}, u32[]{:S(2)}) copy-start(u32[32]{0:T(128)} %constant.59) | copy-start | bytes 388
  187.8 18.4 %all-to-all-start.2 = ((bf16[16,6,2048]{2,1,0:T(8,128)(2,1)}), bf16[16,6,2048]{2,1,0:T(8,128)(2,1)S(1)}, u32[]{:S(2)}, u32[]{:S(2)}) async-start(bf16[16,6,2048]{2,1,0:T(8,128)(2,1)} %copy.37), calls=%async_computation.2 | async-start | bytes 1048576 | tf_op jit(solution)/shard_map/all_to_all | solution.py:122
Sparse Core Ops, SparseCore 0:
  69.0 87.9 all-reduce.4
where the time goes:
time: 224 us; the launch traced here: 223 us
  waiting for transfers between devices  99.8 us (45%)
  blocking collectives  74.4 us (33%)
  between operations  15.6 us (7%)
  matrix products  12.3 us (5%)
  starting transfers between devices  11.6 us (5%)
  other arithmetic  5.19 us (2%)
  local copies, waits for them, and re-layouts  4.47 us (2%)
    unnamed x2, waiting for transfers between devices  87 us
    psum x1, blocking collectives, local(): adapter_down_rows = lax.psum(adapter_output, 'expert')  30 us
    unnamed x2, blocking collectives  20.7 us
    all_to_all x1, blocking collectives, local(): lax.all_to_all(outgoing, 'expert', split_axis=0, concat_axis=0, tiled=True)  19.2 us
    all_to_all x1, waiting for transfers between devices, local(): lax.all_to_all(partial_value.astype(jnp.bfloat16), 'expert', split_axis=0...  12.8 us
    all_to_all x1, starting transfers between devices, local(): lax.all_to_all(latent_out, 'expert', split_axis=1, concat_axis=0, tiled=T...  7.41 us
  transfers between devices with their start and end apart: 3, of which 2 were waited for; matrix products, arithmetic and copies ran while one was open for 1% of the time, Pallas kernels for 0%

commit v1 on v0

--- a/solution.py
+++ b/solution.py
@@ -70,7 +70,7 @@
     adapter_output = jnp.sum(
         jnp.where(chosen_adapters[:, :, None], down_projected_rows, 0.0), axis=1
     )
-    adapter_down_rows = lax.psum(adapter_output, "expert")
+    adapter_down_rows = jnp.sum(lax.all_gather(adapter_output, "expert"), axis=0)
     adapter_scaled_output = (ADAPTER_SCALE * adapter_down_rows).astype(jnp.bfloat16)
     first_owned = lax.axis_index("expert") * owned_count
     holder_mask = (

time: 224 us -> 213 us (0.951)
  blocking collectives: 74.4 us -> 62.7 us
    psum x1 -> x0, blocking collectives: 30 us -> none  [local(): adapter_down_rows = lax.psum(adapter_output, 'expert')]
    all_gather x0 -> x1, blocking collectives: none -> 18.3 us  [local(): lax.all_gather(adapter_output, 'expert')]
where the time goes in v1:
time: 213 us; the launch traced here: 212 us
  waiting for transfers between devices  100 us (47%)
  blocking collectives  62.7 us (29%)
  between operations  15.6 us (7%)
  matrix products  12.3 us (6%)
  starting transfers between devices  11.6 us (5%)
  other arithmetic  5.22 us (2%)
  local copies, waits for them, and re-layouts  4.47 us (2%)
    unnamed x2, waiting for transfers between devices  87.7 us
    unnamed x2, blocking collectives  20.7 us
    all_to_all x1, blocking collectives, local(): lax.all_to_all(outgoing, 'expert', split_axis=0, concat_axis=0, tiled=True)  19.2 us
    all_gather x1, blocking collectives, local(): lax.all_gather(adapter_output, 'expert')  18.3 us
    all_to_all x1, waiting for transfers between devices, local(): lax.all_to_all(partial_value.astype(jnp.bfloat16), 'expert', split_axis=0...  12.8 us
    all_to_all x1, starting transfers between devices, local(): lax.all_to_all(latent_out, 'expert', split_axis=1, concat_axis=0, tiled=T...  7.41 us
    all_gather x1, blocking collectives, local(): column = lax.all_gather(normed, 'dp', axis=0, tiled=True)  4.41 us
  transfers between devices with their start and end apart: 3, of which 2 were waited for; matrix products, arithmetic and copies ran while one was open for 1% of the time, Pallas kernels for 0%

profile of v1, /device:TPU:0, one launch (start us, length us, event | category | flops | bytes accessed | tf_op | source)
XLA Modules:
  0.0 212.4 jit_solution(792038676736914571)
XLA Ops:
  6.5 0.9 iota_compare_fusion.4
  7.4 2.1 %fusion.17 = f32[4,16,512]{2,1,0:T(8,128)S(1)} fusion(bf16[4,16,576]{2,1,0:T(8,128)(2,1)} %param.14, bf16[4,512,576]{1,2,0:T(8,128)(2,1)} %param.15, pred[4,512]{1,0:T(4,128)(4,1)S(1)} %iota_compare_fusion.4), kind=kOutput, calls=%fused_computation.19 | convolution fusion | flops 37814272 | bytes 2566144 | tf_op jit(solution)/shard_map/vmap()/dot_general | solution.py:15
  9.6 0.2 fusion.31
  9.8 2.3 %fusion.19 = bf16[4,16,512]{2,1,0:T(8,128)(2,1)S(1)} fusion(bf16[4,512,576]{1,2,0:T(8,128)(2,1)} %param.15, f32[4,16]{1,0:T(4,128)S(1)} %fusion.31, f32[4,16,512]{2,1,0:T(8,128)S(1)} %fusion.17), kind=kOutput, calls=%fused_computation.21 | convolution fusion | flops 33686080 | bytes 2426880 | tf_op jit(solution)/shard_map/vmap()/dot_general | solution.py:25
  12.1 0.7 copy.29
  12.8 7.4 %all-to-all-start = ((bf16[4,16,512]{2,0,1:T(4,128)(2,1)}), bf16[4,16,512]{2,0,1:T(4,128)(2,1)S(1)}, u32[]{:S(2)}, u32[]{:S(2)}) async-start(bf16[4,16,512]{2,0,1:T(4,128)(2,1)} %copy.29), calls=%async_computation | async-start | bytes 131072 | tf_op jit(solution)/shard_map/all_to_all | solution.py:61
  20.4 0.6 fusion.30
  21.7 0.2 dynamic-update-slice
  21.9 12.4 %all-reduce = s32[64]{0:T(128)S(1)} all-reduce(s32[64]{0:T(128)S(1)} %dynamic-update-slice), channel_id=1, replica_groups=mesh['dp'=2,'expert'=16] {'expert'}, use_global_device_ids=true, to_apply=%add | all-reduce | flops 64 | bytes 512
  34.3 0.2 copy.30
  34.7 0.2 select_reduce_fusion
  35.2 0.5 fusion.16
  35.7 18.3 %all-gather.1 = f32[16,64,16]{1,2,0:T(8,128)S(1)} all-gather(f32[1,64,16]{1,2,0:T(8,128)S(1)} %bitcast.47), channel_id=2, replica_groups=mesh['dp'=2,'expert'=16] {'expert'}, dimensions={0}, use_global_device_ids=true | all-gather | bytes 69632 | tf_op jit(solution)/shard_map/all_gather | solution.py:73
  54.0 2.1 fusion.32
  56.1 1.1 convolution_add_fusion
  57.4 0.1 copy.35
  58.3 87.6 %all-reduce.5.cloned.1.call-done = f32[64,2048]{1,0:T(8,128)} async-done(((f32[64,2048]{1,0:T(8,128)}), f32[64,2048]{1,0:T(8,128)}) %all-reduce.5.cloned.1.call-update) | async-done | bytes 524304
  146.0 1.0 multiply_reduce_fusion
  146.9 0.9 fusion.28
  147.9 4.4 %all-gather.2 = bf16[2,4,2048]{2,1,0:T(4,128)(2,1)S(1)} all-gather(bf16[1,4,2048]{2,1,0:T(4,128)(2,1)S(1)} %fusion.28), channel_id=1, replica_groups=mesh['dp'=2,'expert'=16] {'dp'}, dimensions={0}, use_global_device_ids=true | all-gather | bytes 49152 | tf_op jit(solution)/shard_map/all_gather | solution.py:94
  152.3 0.3 convolution_convert_fusion.1
  152.7 19.2 %all_to_all.26 = bf16[16,6,2048]{2,1,0:T(8,128)(2,1)S(1)} all-to-all(bf16[16,6,2048]{2,1,0:T(8,128)(2,1)S(1)} %reshape.125), channel_id=1, replica_groups=mesh['dp'=2,'expert'=16] {'expert'}, dimensions={0} | all-to-all | bytes 786432 | tf_op jit(solution)/shard_map/all_to_all | solution.py:119
  172.1 2.2 %fusion.5 = f32[96,512]{1,0:T(8,128)S(1)} fusion(bf16[96,2048]{1,0:T(8,128)(2,1)S(1)} %reshape.126, bf16[1,2048,512]{2,1,0:T(8,128)(2,1)} %param.25), kind=kOutput, calls=%fused_computation.9 | convolution fusion | flops 201326592 | bytes 2686976 | tf_op jit(solution)/shard_map/dot_general | solution.py:31
  174.4 0.5 fusion.13
  174.9 0.8 convolution_convert_fusion
  175.7 1.0 copy.37
  176.7 4.2 %all-to-all-start.2 = ((bf16[16,6,2048]{2,1,0:T(8,128)(2,1)}), bf16[16,6,2048]{2,1,0:T(8,128)(2,1)S(1)}, u32[]{:S(2)}, u32[]{:S(2)}) async-start(bf16[16,6,2048]{2,1,0:T(8,128)(2,1)} %copy.37), calls=%async_computation.2 | async-start | bytes 1048576 | tf_op jit(solution)/shard_map/all_to_all | solution.py:122
  181.0 0.6 dynamic-slice.3
  182.3 12.8 %all-to-all-done.2 = bf16[16,6,2048]{2,1,0:T(8,128)(2,1)S(1)} async-done(((bf16[16,6,2048]{2,1,0:T(8,128)(2,1)}), bf16[16,6,2048]{2,1,0:T(8,128)(2,1)S(1)}, u32[]{:S(2)}, u32[]{:S(2)}) %all-to-all-start.2) | async-done | bytes 393248 | tf_op jit(solution)/shard_map/all_to_all | solution.py:122
  195.2 0.6 fusion.1
  195.7 8.3 %all-reduce.2 = bf16[8,2048]{1,0:T(8,128)(2,1)S(1)} all-reduce(bf16[8,2048]{1,0:T(8,128)(2,1)S(1)} %fusion.1), channel_id=4, replica_groups=mesh['dp'=2,'expert'=16] {'dp'}, use_global_device_ids=true, to_apply=%region_10.11.clone | all-reduce | flops 16384 | bytes 65536
  204.1 1.5 add_convert_fusion
  (52 shorter events, 1.6 us)
Async XLA Ops:
  6.5 168.3 %copy-start = (bf16[1,2048,512]{2,1,0:T(8,128)(2,1)S(1)}, bf16[1,2048,512]{2,1,0:T(8,128)(2,1)}, u32[]{:S(2)}) copy-start(bf16[1,2048,512]{2,1,0:T(8,128)(2,1)} %param.27) | copy-start | bytes 6291460
  9.6 10.7 %copy-start.4 = (s32[8,6]{1,0:T(8,128)S(1)}, s32[8,6]{1,0:T(8,128)}, u32[]{:S(2)}) copy-start(s32[8,6]{1,0:T(8,128)} %param.23) | copy-start | bytes 580
  9.6 10.8 %copy-start.7 = (u32[32]{0:T(128)S(1)}, u32[32]{0:T(128)}, u32[]{:S(2)}) copy-start(u32[32]{0:T(128)} %constant.49) | copy-start | bytes 388
  9.6 12.1 %copy-start.9 = (s32[4]{0:T(128)S(1)}, s32[4]{0:T(128)}, u32[]{:S(2)}) copy-start(s32[4]{0:T(128)} %param.18) | copy-start | bytes 52
  9.6 24.7 %copy-start.1 = (bf16[512,512]{1,0:T(8,128)(2,1)S(1)}, bf16[512,512]{1,0:T(8,128)(2,1)}, u32[]{:S(2)}) copy-start(bf16[512,512]{1,0:T(8,128)(2,1)} %param.20) | copy-start | bytes 1572868
  9.6 24.9 %copy-start.5 = (bf16[2048]{0:T(1024)(128)(2,1)S(1)}, bf16[2048]{0:T(1024)(128)(2,1)}, u32[]{:S(2)}) copy-start(bf16[2048]{0:T(1024)(128)(2,1)} %param.22) | copy-start | bytes 12292
  12.8 22.4 %all-to-all-start = ((bf16[4,16,512]{2,0,1:T(4,128)(2,1)}), bf16[4,16,512]{2,0,1:T(4,128)(2,1)S(1)}, u32[]{:S(2)}, u32[]{:S(2)}) async-start(bf16[4,16,512]{2,0,1:T(4,128)(2,1)} %copy.29), calls=%async_computation | async-start | bytes 131072 | tf_op jit(solution)/shard_map/all_to_all | solution.py:61
  20.2 125.8 %all-reduce.5.cloned.1.call-start = ((), (), s32[]{:S(2)}) async-start(), calls=%async_computation.3 | async-start | bytes 1048576
  35.1 21.1 %copy-start.3 = (bf16[32,2048]{1,0:T(8,128)(2,1)S(1)}, bf16[32,2048]{1,0:T(8,128)(2,1)}, u32[]{:S(2)}) copy-start(bf16[32,2048]{1,0:T(8,128)(2,1)} %param.21) | copy-start | bytes 393220
  54.0 91.9 %copy-start.2 = (bf16[4,2048]{1,0:T(4,128)(2,1)S(1)}, bf16[4,2048]{1,0:T(4,128)(2,1)}, u32[]{:S(2)}) copy-start(bf16[4,2048]{1,0:T(4,128)(2,1)} %param.17) | copy-start | bytes 49156
  172.1 2.2 %copy-start.8 = (bf16[1,2048,512]{2,1,0:T(8,128)(2,1)S(1)}, bf16[1,2048,512]{2,1,0:T(8,128)(2,1)}, u32[]{:S(2)}) copy-start(bf16[1,2048,512]{2,1,0:T(8,128)(2,1)} %param.26) | copy-start | bytes 6291460
  174.9 6.0 %copy-start.6 = (f32[8,6]{1,0:T(8,128)S(1)}, f32[8,6]{1,0:T(8,128)}, u32[]{:S(2)}) copy-start(f32[8,6]{1,0:T(8,128)} %param.24) | copy-start | bytes 580
  174.9 6.1 %copy-start.10 = (u32[32]{0:T(128)S(1)}, u32[32]{0:T(128)}, u32[]{:S(2)}) copy-start(u32[32]{0:T(128)} %constant.59) | copy-start | bytes 388
  176.7 18.4 %all-to-all-start.2 = ((bf16[16,6,2048]{2,1,0:T(8,128)(2,1)}), bf16[16,6,2048]{2,1,0:T(8,128)(2,1)S(1)}, u32[]{:S(2)}, u32[]{:S(2)}) async-start(bf16[16,6,2048]{2,1,0:T(8,128)(2,1)} %copy.37), calls=%async_computation.2 | async-start | bytes 1048576 | tf_op jit(solution)/shard_map/all_to_all | solution.py:122
Sparse Core Ops, SparseCore 0:
  57.3 88.5 all-reduce.4
